TPU v7x, 32 devices: a whole 2x2x4 slice. The times are simulated.
32 devices in a mesh: ctx: 8 (over z, core), tp: 4 (over y, x).
Axes of the slice: x: 2, y: 2, z: 4, core: 2. Of those that a mesh axis runs over, the one named last changes fastest.
Arguments:
- hidden_rows: bfloat16 [4096, 8192], P('ctx', 'tp'), may hold values from -6 to 6
- w_value: bfloat16 [8192, 8192], P('ctx', 'tp'), may hold values from -0.0625 to 0.0625
- w_gate: bfloat16 [8192, 8192], P('ctx', 'tp'), may hold values from -0.0625 to 0.0625
- state_proj: bfloat16 [4096, 2, 4, 256], P('ctx'), may hold values from -1.5 to 1.5
- rates: float32 [4096, 128], P('ctx', 'tp'), may hold values from 0 to 4.5, as said below
- read_weights: float32 [6, 4096, 128], P(None, 'ctx', 'tp'), may hold values from 0.25 to 2
- prior_state: float32 [128, 64, 256], P('tp'), may hold values from -24 to 24
- skip_weight: float32 [128], P('tp'), may hold values from 0.5 to 2
- norm_gain: float32 [8192], P('tp'), may hold values from 0.25 to 1.75
Outputs:
- layer_out: bfloat16 [4096, 8192], P('ctx', 'tp')
Inputs may be any that keep to these rules, and one draw needn't show every extreme that they name: Positive rates.
All inputs are finite; a program needn't handle non-finite values.
Results may differ from a plain program's by a relative error of at most 0.0085.
Values may be sent and summed in bfloat16 or wider, within the bound.
A program may use at most 128 MiB of HBM per device.

v0:
```python
import jax
import jax.numpy as jnp
from jax import lax
from jax.sharding import PartitionSpec as P

HEAD_DIM = 64
STATE = 256
HPG = 32
LEVELS = 6


def swapped(value, axis, distance):
    return lax.ppermute(value, axis, [(i, i ^ 1 << distance) for i in range(lax.axis_size(axis))])


def on_device(
    hidden_rows,
    w_value,
    w_gate,
    state_proj,
    rates,
    read_weights,
    prior_state,
    skip_weight,
    norm_gain,
):
    tok_rows = rates.shape[0]
    head_count = rates.shape[1]
    level_total = LEVELS - 2
    ctx_size = lax.axis_size("ctx")
    half = ctx_size // 2
    my_block = lax.axis_index("ctx")
    upper_half = my_block // half
    groups = [list(range(half)), list(range(half, ctx_size))]
    across = [(i, (i + half) % ctx_size) for i in range(ctx_size)]
    w_value_half = lax.all_gather(w_value, "ctx", axis=0, tiled=True, axis_index_groups=groups)
    token_part = lax.all_to_all(hidden_rows, "tp", 0, 1, tiled=True)
    depth = token_part.shape[1] // 2
    kept = lax.dynamic_slice_in_dim(token_part, upper_half * depth, depth, 1)
    given = lax.dynamic_slice_in_dim(token_part, (1 - upper_half) * depth, depth, 1)
    taken = lax.ppermute(given, "ctx", across)
    rows = lax.all_gather(jnp.stack([kept, taken]), "tp", axis=1, tiled=True)
    w_gate_half = lax.all_gather(w_gate, "ctx", axis=0, tiled=True, axis_index_groups=groups)

    def project(weight):
        other = jnp.dot(rows[1], weight, preferred_element_type=jnp.float32).astype(jnp.bfloat16)
        back = lax.ppermute(other, "ctx", across)
        mine = jnp.dot(rows[0], weight, preferred_element_type=jnp.float32)
        return (mine + back.astype(jnp.float32)).astype(jnp.bfloat16)

    values_proj = project(w_value_half)
    gates_proj = project(w_gate_half)
    values3 = values_proj.reshape(tok_rows, head_count, HEAD_DIM)
    group_index = lax.axis_index("tp") * head_count // HPG
    write_vec = lax.dynamic_index_in_dim(state_proj[:, 0], group_index, 1, keepdims=False)
    read_vec = lax.dynamic_index_in_dim(state_proj[:, 1], group_index, 1, keepdims=False)
    cum_rate = jnp.cumsum(rates, axis=0)
    scores = lax.dot_general(
        read_vec, write_vec, (((1,), (1,)), ((), ())), preferred_element_type=jnp.float32
    )
    rate_lag = cum_rate.T[:, :, None] - cum_rate.T[:, None, :]
    causal = (jnp.arange(tok_rows)[:, None] >= jnp.arange(tok_rows)[None, :])[None]
    mixing = (
        jnp.where(causal, jnp.exp(-jnp.where(causal, rate_lag, 0.0)), 0.0) * scores[None]
    ).astype(jnp.bfloat16)
    local_out = jnp.einsum("hts,shp->thp", mixing, values3, preferred_element_type=jnp.float32)
    span_total = cum_rate[-1]
    write_weighted = (
        jnp.exp(-(span_total[None] - cum_rate))[:, :, None]
        * write_vec[:, None, :].astype(jnp.float32)
    ).astype(jnp.bfloat16)
    end_state = jnp.einsum(
        "thn,thp->hpn", write_weighted, values3, preferred_element_type=jnp.float32
    )
    agg_state = end_state
    agg_rate = span_total
    start_rate = jnp.zeros((head_count,), jnp.float32)
    tier_components = []
    bits = ctx_size.bit_length() - 1
    for bit_pos in range(bits):
        is_upper = jnp.right_shift(my_block, bit_pos) % 2 == 1
        if bit_pos < bits - 1:
            other_state, other_rate = swapped(
                (agg_state.astype(jnp.bfloat16), agg_rate), "ctx", bit_pos
            )
        else:
            share = head_count // half
            piece = lax.dynamic_slice_in_dim(
                agg_state.astype(jnp.bfloat16), my_block % half * share, share, 0
            )
            piece, other_rate = swapped((piece, agg_rate), "ctx", bit_pos)
            other_state = lax.all_gather(piece, "ctx", axis=0, tiled=True, axis_index_groups=groups)
        other_state = other_state.astype(jnp.float32)
        tier_components.append(
            jnp.where(is_upper, other_state * jnp.exp(-start_rate)[:, None, None], 0.0).astype(
                jnp.bfloat16
            )
        )
        if bit_pos < bits - 1:
            agg_state = jnp.where(
                is_upper,
                other_state * jnp.exp(-agg_rate)[:, None, None] + agg_state,
                agg_state * jnp.exp(-other_rate)[:, None, None] + other_state,
            )
            agg_rate = agg_rate + other_rate
        start_rate = jnp.where(is_upper, start_rate + other_rate, start_rate)
    level_ids = list(range(1, 1 + len(tier_components))) + [level_total + 1]
    prior_part = (jnp.exp(-start_rate)[:, None, None] * prior_state).astype(jnp.bfloat16)
    carried_out = 0.0
    for level, state in zip(level_ids, tier_components + [prior_part]):
        projected = lax.dot_general(
            read_vec, state, (((1,), (2,)), ((), ())), preferred_element_type=jnp.float32
        )
        carried_out = carried_out + read_weights[level][:, :, None] * projected
    carried_out = carried_out * jnp.exp(-cum_rate)[:, :, None]
    mixed_out = (
        read_weights[0][:, :, None] * local_out
        + carried_out
        + skip_weight[None, :, None] * values3.astype(jnp.float32)
    )
    gates3 = gates_proj.reshape(tok_rows, head_count, HEAD_DIM).astype(jnp.float32)
    filtered_result = mixed_out * jax.nn.silu(gates3)
    inverse = lax.rsqrt(jnp.mean(filtered_result * filtered_result, axis=2, keepdims=True) + 1e-05)
    result = filtered_result * inverse * norm_gain.reshape(head_count, HEAD_DIM)[None]
    return result.reshape(tok_rows, head_count * HEAD_DIM).astype(jnp.bfloat16)


def solution(mesh):
    in_specs = (
        P("ctx", "tp"),
        P("ctx", "tp"),
        P("ctx", "tp"),
        P("ctx", None, None, None),
        P("ctx", "tp"),
        P(None, "ctx", "tp"),
        P("tp", None, None),
        P("tp"),
        P("tp"),
    )
    out_specs = P("ctx", "tp")
    return jax.shard_map(
        on_device, mesh=mesh, in_specs=in_specs, out_specs=out_specs, check_vma=False
    )
```

profile of v0, /device:TPU:9, one launch (start us, length us, event | category | flops | bytes accessed | tf_op | source)
XLA Modules:
  0.0 692.2 jit_solution(7974122275637715766)
XLA Ops:
  6.5 3.7 all-to-all-start
  10.4 24.3 %all-to-all-done = bf16[4,128,2048]{2,1,0:T(8,128)(2,1)S(1)} async-done(((bf16[4,128,2048]{2,1,0:T(8,128)(2,1)}), bf16[4,128,2048]{2,1,0:T(8,128)(2,1)S(1)}, u32[]{:S(2)}, u32[]{:S(2)}) %all-to-all-start) | async-done | bytes 2097184 | tf_op jit(solution)/shard_map/all_to_all | solution.py:37
  34.6 1.3 copy-done.2
  36.0 3.0 copy.35
  39.1 2.4 collective-permute-start
  41.5 45.2 %collective-permute-done = bf16[128,4096]{0,1:T(8,128)(2,1)S(1)} collective-permute-done((bf16[128,4096]{0,1:T(8,128)(2,1)S(1)}, bf16[128,4096]{0,1:T(8,128)(2,1)S(1)}, u32[]{:S(2)}, u32[]{:S(2)}) %collective-permute-start) | collective-permute-done | bytes 1048608 | tf_op jit(solution)/shard_map/ppermute | solution.py:41
  86.8 1.5 pad_maximum_fusion
  88.3 0.7 all-gather.7.cloned.1.call-update
  89.1 0.7 all-gather.11.cloned.1.call-update
  89.8 86.4 %all-gather.5.cloned.1.call-done = bf16[2,512,4096]{1,2,0:T(8,128)(2,1)} async-done(((bf16[2,128,4096]{1,2,0:T(8,128)(2,1)}), bf16[2,512,4096]{1,2,0:T(8,128)(2,1)}) %all-gather.5.cloned.1.call-update) | async-done | bytes 8388624 | tf_op jit(solution)/shard_map/all_gather | solution.py:42
  176.2 149.6 %all-gather.7.cloned.1.call-done = bf16[4096,2048]{1,0:T(8,128)(2,1)} async-done(((bf16[1024,2048]{1,0:T(8,128)(2,1)}), bf16[4096,2048]{1,0:T(8,128)(2,1)}) %all-gather.7.cloned.1.call-update) | async-done | bytes 16777232 | tf_op jit(solution)/shard_map/all_gather | solution.py:36
  325.8 14.6 %fusion.12 = bf16[512,2048]{1,0:T(8,128)(2,1)} fusion(bf16[4096,2048]{1,0:T(8,128)(2,1)} %all-gather.7.cloned.1.call-done, bf16[2,512,4096]{1,2,0:T(8,128)(2,1)} %all-gather.5.cloned.1.call-done), kind=kOutput, calls=%fused_computation.24 | convolution fusion | flops 8590983168 | bytes 23068672 | tf_op jit(solution)/shard_map/dot_general | solution.py:46
  340.4 2.3 collective-permute-start.1
  342.8 1.2 reduce-window.6
  344.1 0.7 copy_bitcast_fusion.2
  345.0 2.4 fusion.50
  347.4 0.5 constant_dynamic-slice_fusion
  348.1 85.4 %collective-permute-done.1 = bf16[512,2048]{1,0:T(8,128)(2,1)} collective-permute-done((bf16[512,2048]{1,0:T(8,128)(2,1)}, bf16[512,2048]{1,0:T(8,128)(2,1)}, u32[]{:S(2)}, u32[]{:S(2)}) %collective-permute-start.1) | collective-permute-done | bytes 2097184 | tf_op jit(solution)/shard_map/ppermute | solution.py:47
  433.5 15.1 %add_convert_fusion.1 = bf16[512,2048]{1,0:T(8,128)(2,1)} fusion(bf16[512,2048]{1,0:T(8,128)(2,1)} %collective-permute-done.1, bf16[4096,2048]{1,0:T(8,128)(2,1)} %all-gather.7.cloned.1.call-done, bf16[2,512,4096]{1,2,0:T(8,128)(2,1)} %all-gather.5.cloned.1.call-done), kind=kOutput, calls=%fused_computation.16 | convolution fusion | flops 8593080320 | bytes 25165824 | tf_op jit(solution)/shard_map/dot_general | solution.py:48
  448.7 4.0 copy.36
  452.6 5.1 fusion.51
  457.7 0.4 collective-permute-start.2
  458.1 62.8 %all-gather.11.cloned.1.call-done = bf16[4096,2048]{1,0:T(8,128)(2,1)} async-done(((bf16[1024,2048]{1,0:T(8,128)(2,1)}), bf16[4096,2048]{1,0:T(8,128)(2,1)}) %all-gather.11.cloned.1.call-update) | async-done | bytes 16777232 | tf_op jit(solution)/shard_map/all_gather | solution.py:43
  520.9 14.6 %fusion.13 = bf16[512,2048]{1,0:T(8,128)(2,1)} fusion(bf16[4096,2048]{1,0:T(8,128)(2,1)} %all-gather.11.cloned.1.call-done, bf16[2,512,4096]{1,2,0:T(8,128)(2,1)} %all-gather.5.cloned.1.call-done), kind=kOutput, calls=%fused_computation.25 | convolution fusion | flops 8590983168 | bytes 23068672 | tf_op jit(solution)/shard_map/dot_general | solution.py:46
  535.4 2.3 collective-permute-start.8
  537.8 0.5 constant_dynamic-slice_fusion.1
  538.5 0.5 collective-permute-done.3
  538.9 2.2 fusion.48
  541.1 1.3 collective-permute-start.4
  542.4 0.8 iota_compare_fusion
  543.2 0.7 slice_bitcast_fusion.20
  543.9 1.3 fusion.37
  545.2 0.3 collective-permute-start.5
  545.6 61.4 %collective-permute-done.5 = f32[32]{0:T(128)S(1)} collective-permute-done((f32[32]{0:T(128)S(1)}, f32[32]{0:T(128)S(1)}, u32[]{:S(2)}, u32[]{:S(2)}) %collective-permute-start.5) | collective-permute-done | bytes 160 | tf_op jit(solution)/shard_map/ppermute | solution.py:13
  607.0 0.6 negate_exponential_fusion.2
  607.7 20.8 %collective-permute-done.7 = f32[32]{0:T(128)S(1)} collective-permute-done((f32[32]{0:T(128)S(1)}, f32[32]{0:T(128)S(1)}, u32[]{:S(2)}, u32[]{:S(2)}) %collective-permute-start.7) | collective-permute-done | bytes 160 | tf_op jit(solution)/shard_map/ppermute | solution.py:13
  628.5 0.5 fusion.41
  629.5 3.0 collective-permute-start.6
  632.5 15.3 %fusion.14 = f32[512,2048]{1,0:T(8,128)} fusion(bf16[512,2048]{1,0:T(8,128)(2,1)} %collective-permute-done.8, bf16[4096,2048]{1,0:T(8,128)(2,1)} %all-gather.11.cloned.1.call-done, bf16[2,512,4096]{1,2,0:T(8,128)(2,1)} %all-gather.5.cloned.1.call-done), kind=kOutput, calls=%fused_computation.26 | convolution fusion | flops 8594128896 | bytes 27262976 | tf_op jit(solution)/shard_map/dot_general | solution.py:48
  647.9 12.0 %fusion = f32[32,64,512]{2,1,0:T(8,128)} fusion(bf16[512,32,64]{0,2,1:T(8,128)(2,1)} %bitcast.101, f32[512,512]{1,0:T(8,128)S(1)} %copy-done.5, f32[32,512]{1,0:T(8,128)S(1)} %copy-done.7, pred[512,512]{1,0:T(8,128)(4,1)} %iota_compare_fusion), kind=kOutput, calls=%fused_computation.2 | convolution fusion | flops 1124073472 | bytes 7667712 | tf_op jit(solution)/shard_map/hts,shp->thp/dot_general | solution.py:66
  659.9 5.5 copy.41
  665.4 2.7 fusion.21
  668.1 2.8 fusion.18
  671.0 2.1 fusion.19
  673.1 1.0 copy-done.3
  674.1 8.6 %multiply_reduce_fusion = (f32[512,32]{0,1:T(8,128)S(1)}, f32[512,32,64]{0,2,1:T(8,128)S(1)}) fusion(f32[32]{0:T(128)S(1)} %copy-done.17, f32[512,32]{0,1:T(8,128)S(1)} %get-tuple-element.25, f32[512,32]{0,1:T(8,128)S(1)} %copy-done.11, f32[512,32,64]{0,2,1:T(8,128)S(1)} %fusion.19, f32[512,32]{0,1:T(8,128)S(1)} %copy-done.12, f32[512,32,64]{0,2,1:T(8,128)} %fusion.18, ...), kind=kOutput, calls=%fused_computation.14 | convolution fusion | flops 558874624 | bytes 30081280 | tf_op jit(solution)/shard_map/dot_general | solution.py:111
  682.8 0.5 multiply_convert_fusion.4
  683.3 2.4 copy.42
  (63 shorter events, 1.7 us)
Async XLA Ops:
  6.5 336.2 %copy-start = (f32[512,32]{0,1:T(8,128)S(1)}, f32[512,32]{0,1:T(8,128)}, u32[]{:S(2)}) copy-start(f32[512,32]{0,1:T(8,128)} %param.13) | copy-start | bytes 196612
  6.5 28.1 %all-to-all-start = ((bf16[4,128,2048]{2,1,0:T(8,128)(2,1)}), bf16[4,128,2048]{2,1,0:T(8,128)(2,1)S(1)}, u32[]{:S(2)}, u32[]{:S(2)}) async-start(bf16[4,128,2048]{2,1,0:T(8,128)(2,1)} %bitcast.99), calls=%async_computation | async-start | bytes 4194304 | tf_op jit(solution)/shard_map/all_to_all | solution.py:37
  10.3 165.9 %all-gather.5.cloned.1.call-start = ((), (), s32[]{:S(2)}) async-start(), calls=%async_computation.1 | async-start | bytes 10485760 | tf_op jit(solution)/shard_map/all_gather | solution.py:42
  34.6 1.3 copy-start.2
  39.1 47.6 %collective-permute-start = (bf16[128,4096]{0,1:T(8,128)(2,1)S(1)}, bf16[128,4096]{0,1:T(8,128)(2,1)S(1)}, u32[]{:S(2)}, u32[]{:S(2)}) collective-permute-start(bf16[128,4096]{0,1:T(8,128)(2,1)S(1)} %get-tuple-element.16), channel_id=1, source_target_pairs={{0,16},{4,20},{8,24},{12,28},{16,0},{20,4},{24,8},{28,12},{1,17},{... | collective-permute-start | bytes 3145736 | tf_op jit(solution)/shard_map/ppermute | solution.py:41
  88.3 237.6 %all-gather.7.cloned.1.call-start = ((), (), s32[]{:S(2)}) async-start(), calls=%async_computation.2 | async-start | bytes 20971520 | tf_op jit(solution)/shard_map/all_gather | solution.py:36
  89.0 431.8 %all-gather.11.cloned.1.call-start = ((), (), s32[]{:S(2)}) async-start(), calls=%async_computation.4 | async-start | bytes 20971520 | tf_op jit(solution)/shard_map/all_gather | solution.py:43
  89.8 581.2 %all-gather.9.cloned.1.call-start = ((), (), s32[]{:S(2)}) async-start(), calls=%async_computation.3 | async-start | bytes 1310720 | tf_op jit(solution)/shard_map/all_gather | solution.py:92
  340.4 93.1 %collective-permute-start.1 = (bf16[512,2048]{1,0:T(8,128)(2,1)}, bf16[512,2048]{1,0:T(8,128)(2,1)}, u32[]{:S(2)}, u32[]{:S(2)}) collective-permute-start(bf16[512,2048]{1,0:T(8,128)(2,1)} %fusion.12), channel_id=1, source_target_pairs={{0,16},{4,20},{8,24},{12,28},{16,0},{20,4},{24,8},{28,12},{1,17},{... | collective-permute-start | bytes 6291464 | tf_op jit(solution)/shard_map/ppermute | solution.py:47
  457.7 80.7 %copy-start.15 = (f32[2048]{0:T(1024)S(1)}, f32[2048]{0:T(1024)}, u32[]{:S(2)}) copy-start(f32[2048]{0:T(1024)} %param.17) | copy-start | bytes 24580
  457.7 81.2 %collective-permute-start.2 = (bf16[32,64,256]{2,1,0:T(8,128)(2,1)}, bf16[32,64,256]{2,1,0:T(8,128)(2,1)S(1)}, u32[]{:S(2)}, u32[]{:S(2)}) collective-permute-start(bf16[32,64,256]{2,1,0:T(8,128)(2,1)} %get-tuple-element.31), channel_id=1, source_target_pairs={{0,4},{4,0},{8,12},{12,8},{16,20},{20,16},{24,28},{28,24},{1,5},{5... | collective-permute-start | bytes 3145736 | tf_op jit(solution)/shard_map/ppermute | solution.py:13
  535.4 97.1 %collective-permute-start.8 = (bf16[512,2048]{1,0:T(8,128)(2,1)}, bf16[512,2048]{1,0:T(8,128)(2,1)}, u32[]{:S(2)}, u32[]{:S(2)}) collective-permute-start(bf16[512,2048]{1,0:T(8,128)(2,1)} %fusion.13), channel_id=1, source_target_pairs={{0,16},{4,20},{8,24},{12,28},{16,0},{20,4},{24,8},{28,12},{1,17},{... | collective-permute-start | bytes 6291464 | tf_op jit(solution)/shard_map/ppermute | solution.py:47
  537.8 1.2 collective-permute-start.3
  537.8 5.4 copy-start.6
  541.1 87.9 %collective-permute-start.4 = (bf16[32,64,256]{2,1,0:T(8,128)(2,1)S(1)}, bf16[32,64,256]{2,1,0:T(8,128)(2,1)S(1)}, u32[]{:S(2)}, u32[]{:S(2)}) collective-permute-start(bf16[32,64,256]{2,1,0:T(8,128)(2,1)S(1)} %get-tuple-element.11), channel_id=1, source_target_pairs={{0,8},{4,12},{8,0},{12,4},{16,24},{20,28},{24,16},{28,20},{1,9},{5... | collective-permute-start | bytes 3145736 | tf_op jit(solution)/shard_map/ppermute | solution.py:13
  545.2 61.8 %collective-permute-start.5 = (f32[32]{0:T(128)S(1)}, f32[32]{0:T(128)S(1)}, u32[]{:S(2)}, u32[]{:S(2)}) collective-permute-start(f32[32]{0:T(128)S(1)} %get-tuple-element.10), channel_id=1, source_target_pairs={{0,8},{4,12},{8,0},{12,4},{16,24},{20,28},{24,16},{28,20},{1,9},{5... | collective-permute-start | bytes 392 | tf_op jit(solution)/shard_map/ppermute | solution.py:13
  607.6 20.9 %collective-permute-start.7 = (f32[32]{0:T(128)S(1)}, f32[32]{0:T(128)S(1)}, u32[]{:S(2)}, u32[]{:S(2)}) collective-permute-start(f32[32]{0:T(128)S(1)} %get-tuple-element.28), channel_id=1, source_target_pairs={{0,16},{4,20},{8,24},{12,28},{16,0},{20,4},{24,8},{28,12},{1,17},{... | collective-permute-start | bytes 392 | tf_op jit(solution)/shard_map/ppermute | solution.py:13
  629.4 18.4 %copy-start.5 = (f32[512,512]{1,0:T(8,128)S(1)}, f32[512,512]{1,0:T(8,128)}, u32[]{:S(2)}) copy-start(f32[512,512]{1,0:T(8,128)} %fusion.37) | copy-start | bytes 3145732
  629.5 18.4 %copy-start.7 = (f32[32,512]{1,0:T(8,128)S(1)}, f32[32,512]{1,0:T(8,128)}, u32[]{:S(2)}) copy-start(f32[32,512]{1,0:T(8,128)} %get-tuple-element.22) | copy-start | bytes 196612
  629.5 18.4 %collective-permute-start.6 = (bf16[8,64,256]{2,1,0:T(8,128)(2,1)S(1)}, bf16[8,64,256]{2,1,0:T(8,128)(2,1)}, u32[]{:S(2)}, u32[]{:S(2)}) collective-permute-start(bf16[8,64,256]{2,1,0:T(8,128)(2,1)S(1)} %select_convert_fusion.4), channel_id=1, source_target_pairs={{0,16},{4,20},{8,24},{12,28},{16,0},{20,4},{24,8},{28,12},{1,17},{... | collective-permute-start | bytes 786440 | tf_op jit(solution)/shard_map/ppermute | solution.py:13
  665.4 2.7 copy-start.14
  668.1 2.8 copy-start.13
  668.1 5.0 copy-start.11
  668.1 5.0 copy-start.12
  670.9 2.2 copy-start.4
  670.9 2.2 copy-start.8
  670.9 2.2 copy-start.9
  670.9 2.2 copy-start.10
  670.9 2.3 copy-start.16
  670.9 2.3 copy-start.17
  670.9 3.2 copy-start.3
  682.7 2.9 copy-start.1
Sparse Core Ops, SparseCore 0:
  88.4 87.7 all-gather.4
  177.8 148.0 all-gather.6
  327.4 193.4 all-gather.10
  648.0 17.0 all-gather.8
where the time goes:
time: 693 us; the launch traced here: 692 us
  waiting for transfers between devices  538 us (78%)
  matrix products  94.2 us (14%)
  local copies, waits for them, and re-layouts  22.1 us (3%)
  starting transfers between devices  15.9 us (2%)
  between operations  13.5 us (2%)
  other arithmetic  8.63 us (1%)
    all_gather x1, waiting for transfers between devices, on_device(): lax.all_gather(w_value, 'ctx', axis=0, tiled=True, axis_index_groups=groups)  150 us
    all_gather x1, waiting for transfers between devices, on_device(): rows = lax.all_gather(jnp.stack([kept, taken]), 'tp', axis=1, tiled=True)  86.4 us
    ppermute x2, waiting for transfers between devices, project(): back = lax.ppermute(other, 'ctx', across)  85.4 us
    ppermute x6, waiting for transfers between devices, swapped(): lax.ppermute(value, axis, [(i, i ^ 1 << distance) for i in range(lax.axis...  82.7 us
    all_gather x1, waiting for transfers between devices, on_device(): lax.all_gather(w_gate, 'ctx', axis=0, tiled=True, axis_index_groups=groups)  62.8 us
    ppermute x1, waiting for transfers between devices, on_device(): taken = lax.ppermute(given, 'ctx', across)  45.2 us
    dot_general x2, matrix products, project(): mine = jnp.dot(rows[0], weight, preferred_element_type=jnp.float32)  30.5 us
    dot_general x2, matrix products, project(): jnp.dot(rows[1], weight, preferred_element_type=jnp.float32)  29.2 us
  transfers between devices with their start and end apart: 14, of which 9 were waited for; matrix products, arithmetic and copies ran while one was open for 15% of the time, Pallas kernels for 0%

commit v1 on v0

--- a/solution.py
+++ b/solution.py
@@ -7,6 +7,24 @@
 STATE = 256
 HPG = 32
 LEVELS = 6
+
+
+def in_order(blocks, dim):
+    dims = list(blocks.shape[1:])
+    dims[dim] *= blocks.shape[0]
+    return jnp.moveaxis(blocks, 0, dim).reshape(dims)
+
+
+def collected_by_bits(value, axis):
+    size = lax.axis_size(axis)
+    parts = value[None]
+    for level in range(size.bit_length() - 1):
+        bit = 1 << level
+        other = lax.ppermute(parts, axis, [(i, i ^ bit) for i in range(size)])
+        both = jnp.stack([parts, other])
+        upper = lax.axis_index(axis) >> level & 1
+        parts = jnp.where(upper == 0, both, both[::-1]).reshape(-1, *value.shape)
+    return parts
 
 
 def swapped(value, axis, distance):
@@ -39,7 +57,8 @@
     kept = lax.dynamic_slice_in_dim(token_part, upper_half * depth, depth, 1)
     given = lax.dynamic_slice_in_dim(token_part, (1 - upper_half) * depth, depth, 1)
     taken = lax.ppermute(given, "ctx", across)
-    rows = lax.all_gather(jnp.stack([kept, taken]), "tp", axis=1, tiled=True)
+    x = jnp.stack([kept, taken])
+    rows = in_order(collected_by_bits(x, "tp"), 1)
     w_gate_half = lax.all_gather(w_gate, "ctx", axis=0, tiled=True, axis_index_groups=groups)
 
     def project(weight):

time: 693 us -> 579 us (0.84)
  waiting for transfers between devices: 538 us -> 377 us
  other arithmetic: 8.63 us -> 34.1 us
  local copies, waits for them, and re-layouts: 22.1 us -> 39.1 us
    all_gather x1, waiting for transfers between devices: 150 us -> 0.01 us  [on_device(): lax.all_gather(w_value, 'ctx', axis=0, tiled=True, axis_index_groups=groups)]
    ppermute x0 -> x2, waiting for transfers between devices: none -> 134 us  [collected_by_bits(): other = lax.ppermute(parts, axis, [(i, i ^ bit) for i in range(size)])]
    all_gather x1 -> x0, waiting for transfers between devices: 86.4 us -> none  [on_device(): rows = lax.all_gather(jnp.stack([kept, taken]), 'tp', axis=1, tiled=True)]
    all_gather x1, waiting for transfers between devices: 62.8 us -> 0.01 us  [on_device(): lax.all_gather(w_gate, 'ctx', axis=0, tiled=True, axis_index_groups=groups)]
    another operation x4 -> x7, other arithmetic: 3.42 us -> 17 us  [the longest x4 15.7 us: collected_by_bits(): both = jnp.stack([parts, other])]
    reshape x1 -> x2, local copies, waits for them, and re-layouts: 0.01 us -> 11.7 us  [the longest x1 11.7 us: collected_by_bits(): parts = jnp.where(upper == 0, both, both[::-1]).reshape(-1, *value.shape)]
    select_n x0 -> x1, other arithmetic: none -> 11.4 us  [collected_by_bits(): parts = jnp.where(upper == 0, both, both[::-1]).reshape(-1, *value.shape)]
    ppermute x6, waiting for transfers between devices: 82.7 us -> 90.4 us  [swapped(): lax.ppermute(value, axis, [(i, i ^ 1 << distance) for i in range(lax.axis...]
  transfers between devices with their start and end apart: 14 -> 15, of which waited for: 9 -> 8; matrix products, arithmetic and copies ran while one was open for 15% -> 25% of each run, Pallas kernels for 0% -> 0%
where the time goes in v1:
time: 579 us; the launch traced here: 574 us
  waiting for transfers between devices  377 us (65%)
  matrix products  90.8 us (16%)
  local copies, waits for them, and re-layouts  39.1 us (7%)
  other arithmetic  34.1 us (6%)
  starting transfers between devices  19.7 us (3%)
  between operations  13.4 us (2%)
    ppermute x2, waiting for transfers between devices, collected_by_bits(): other = lax.ppermute(parts, axis, [(i, i ^ bit) for i in range(size)])  134 us
    ppermute x6, waiting for transfers between devices, swapped(): lax.ppermute(value, axis, [(i, i ^ 1 << distance) for i in range(lax.axis...  90.4 us
    ppermute x2, waiting for transfers between devices, project(): back = lax.ppermute(other, 'ctx', across)  81.3 us
    ppermute x1, waiting for transfers between devices, on_device(): taken = lax.ppermute(given, 'ctx', across)  45.9 us
    dot_general x2, matrix products, project(): mine = jnp.dot(rows[0], weight, preferred_element_type=jnp.float32)  30.5 us
    dot_general x2, matrix products, project(): jnp.dot(rows[1], weight, preferred_element_type=jnp.float32)  29.5 us
    all_to_all x1, waiting for transfers between devices, on_device(): token_part = lax.all_to_all(hidden_rows, 'tp', 0, 1, tiled=True)  24.4 us
    another operation x4, other arithmetic, collected_by_bits(): both = jnp.stack([parts, other])  15.7 us
  transfers between devices with their start and end apart: 15, of which 8 were waited for; matrix products, arithmetic and copies ran while one was open for 25% of the time, Pallas kernels for 0%

profile of v1, /device:TPU:9, one launch (start us, length us, event | category | flops | bytes accessed | tf_op | source)
XLA Modules:
  0.0 574.3 jit_solution(6333102544470997937)
XLA Ops:
  6.5 0.7 all-gather.4.cloned.1.call-update
  8.0 3.6 all-to-all-start
  11.7 24.4 %all-to-all-done = bf16[4,128,2048]{2,1,0:T(8,128)(2,1)S(1)} async-done(((bf16[4,128,2048]{2,1,0:T(8,128)(2,1)}), bf16[4,128,2048]{2,1,0:T(8,128)(2,1)S(1)}, u32[]{:S(2)}, u32[]{:S(2)}) %all-to-all-start) | async-done | bytes 2097184 | tf_op jit(solution)/shard_map/all_to_all | solution.py:55
  36.1 1.3 copy-done.2
  37.4 3.1 copy.37
  40.7 2.3 collective-permute-start
  43.0 45.9 %collective-permute-done = bf16[128,4096]{0,1:T(8,128)(2,1)S(1)} collective-permute-done((bf16[128,4096]{0,1:T(8,128)(2,1)S(1)}, bf16[128,4096]{0,1:T(8,128)(2,1)S(1)}, u32[]{:S(2)}, u32[]{:S(2)}) %collective-permute-start) | collective-permute-done | bytes 1048608 | tf_op jit(solution)/shard_map/ppermute | solution.py:59
  88.9 1.6 fusion.15
  91.1 45.0 %collective-permute-done.1 = bf16[1,2,128,4096]{2,3,1,0:T(8,128)(2,1)} collective-permute-done((bf16[1,2,128,4096]{2,3,1,0:T(8,128)(2,1)}, bf16[1,2,128,4096]{2,3,1,0:T(8,128)(2,1)}, u32[]{:S(2)}, u32[]{:S(2)}) %collective-permute-start.1) | collective-permute-done | bytes 2097184 | tf_op jit(solution)/shard_map/ppermute | solution.py:23
  136.0 2.0 pad_maximum_fusion.1
  138.0 4.4 fusion.9
  143.1 89.0 %collective-permute-done.2 = bf16[2,2,128,4096]{2,3,1,0:T(8,128)(2,1)} collective-permute-done((bf16[2,2,128,4096]{2,3,1,0:T(8,128)(2,1)}, bf16[2,2,128,4096]{2,3,1,0:T(8,128)(2,1)}, u32[]{:S(2)}, u32[]{:S(2)}) %collective-permute-start.2) | collective-permute-done | bytes 4194336 | tf_op jit(solution)/shard_map/ppermute | solution.py:23
  232.1 7.7 %pad_maximum_fusion = bf16[2,2,2,128,4096]{3,4,2,1,0:T(8,128)(2,1)} fusion(bf16[1,2,2,128,4096]{3,4,2,1,0:T(8,128)(2,1)} %bitcast.11, bf16[1,2,2,128,4096]{3,4,2,1,0:T(8,128)(2,1)} %get-tuple-element.13), kind=kLoop, calls=%fused_computation.6 | loop fusion | flops 4194304 | bytes 16777216 | tf_op jit(solution)/shard_map/stack | solution.py:24
  239.8 11.4 %reverse_select_fusion = bf16[2,2,2,128,4096]{3,4,2,1,0:T(8,128)(2,1)} fusion(bf16[2,2,2,128,4096]{3,4,2,1,0:T(8,128)(2,1)} %pad_maximum_fusion, pred[]{:T(512)S(6)} %eq.20), kind=kLoop, calls=%fused_computation.4 | loop fusion | flops 4194304 | bytes 16777216 | tf_op jit(solution)/shard_map/jit(_where)/select_n | solution.py:26
  251.2 11.7 %copy.38 = bf16[4,2,128,4096]{3,2,0,1:T(8,128)(2,1)} copy(bf16[4,2,128,4096]{2,3,1,0:T(8,128)(2,1)} %bitcast.91) | data formatting | bytes 16777216 | tf_op jit(solution)/shard_map/reshape | solution.py:26
  262.9 6.1 %fusion.47 = (bf16[1,4,128,4096]{3,2,1,0:T(8,128)(2,1)}, bf16[1,4,128,4096]{3,2,1,0:T(8,128)(2,1)}) fusion(bf16[2,4,128,4096]{3,2,1,0:T(8,128)(2,1)} %bitcast.92), kind=kLoop, calls=%fused_computation.94 | loop fusion | bytes 16777216 | tf_op jit(solution)/shard_map/slice | solution.py:65
  269.0 14.8 %convolution_convert_fusion.1 = bf16[512,2048]{1,0:T(8,128)(2,1)} fusion(bf16[512,4096]{1,0:T(8,128)(2,1)} %bitcast.99, bf16[4096,2048]{1,0:T(8,128)(2,1)} %all-gather.4.cloned.1.call-done), kind=kOutput, calls=%fused_computation.25 | convolution fusion | flops 8590983168 | bytes 23068672 | tf_op jit(solution)/shard_map/dot_general | solution.py:65
  283.8 1.2 reduce-window.6
  285.9 3.6 collective-permute-start.5
  289.5 0.7 fusion.48
  290.9 0.8 mul.230
  292.2 1.4 negate_exponential_fusion
  293.6 81.3 %collective-permute-done.3 = bf16[512,2048]{1,0:T(8,128)(2,1)} collective-permute-done((bf16[512,2048]{1,0:T(8,128)(2,1)}, bf16[512,2048]{1,0:T(8,128)(2,1)}, u32[]{:S(2)}, u32[]{:S(2)}) %collective-permute-start.3) | collective-permute-done | bytes 2097184 | tf_op jit(solution)/shard_map/ppermute | solution.py:66
  374.9 14.9 %add_convert_fusion.1 = bf16[512,2048]{1,0:T(8,128)(2,1)} fusion(bf16[512,2048]{1,0:T(8,128)(2,1)} %collective-permute-done.3, bf16[512,4096]{1,0:T(8,128)(2,1)} %bitcast.97, bf16[4096,2048]{1,0:T(8,128)(2,1)} %all-gather.4.cloned.1.call-done), kind=kOutput, calls=%fused_computation.18 | convolution fusion | flops 8593080320 | bytes 25165824 | tf_op jit(solution)/shard_map/dot_general | solution.py:67
  389.8 2.9 copy.39
  392.7 4.2 fusion.49
  396.9 3.0 collective-permute-start.4
  399.9 14.7 %convolution_convert_fusion = bf16[512,2048]{1,0:T(8,128)(2,1)} fusion(bf16[512,4096]{1,0:T(8,128)(2,1)} %bitcast.100, bf16[4096,2048]{1,0:T(8,128)(2,1)} %all-gather.8.cloned.1.call-done), kind=kOutput, calls=%fused_computation.24 | convolution fusion | flops 8590983168 | bytes 23068672 | tf_op jit(solution)/shard_map/dot_general | solution.py:65
  416.4 0.8 iota_compare_fusion
  417.2 0.7 slice_bitcast_fusion.4
  418.0 1.3 fusion.35
  419.3 1.0 collective-permute-start.7
  420.4 63.2 %collective-permute-done.7 = f32[32]{0:T(128)S(1)} collective-permute-done((f32[32]{0:T(128)S(1)}, f32[32]{0:T(128)S(1)}, u32[]{:S(2)}, u32[]{:S(2)}) %collective-permute-start.7) | collective-permute-done | bytes 160 | tf_op jit(solution)/shard_map/ppermute | solution.py:31
  483.6 1.2 negate_exponential_fusion.2
  484.7 1.2 collective-permute-start.9
  486.0 19.1 %collective-permute-done.9 = f32[32]{0:T(128)S(1)} collective-permute-done((f32[32]{0:T(128)S(1)}, f32[32]{0:T(128)S(1)}, u32[]{:S(2)}, u32[]{:S(2)}) %collective-permute-start.9) | collective-permute-done | bytes 160 | tf_op jit(solution)/shard_map/ppermute | solution.py:31
  505.6 3.2 collective-permute-start.8
  508.8 2.7 fusion.18
  511.5 8.0 %collective-permute-done.8 = bf16[8,64,256]{2,1,0:T(8,128)(2,1)S(1)} collective-permute-done((bf16[8,64,256]{2,1,0:T(8,128)(2,1)S(1)}, bf16[8,64,256]{2,1,0:T(8,128)(2,1)S(1)}, u32[]{:S(2)}, u32[]{:S(2)}) %collective-permute-start.8) | collective-permute-done | bytes 262176 | tf_op jit(solution)/shard_map/ppermute | solution.py:31
  519.5 0.7 copy-done.11
  520.2 15.6 %fusion.13 = f32[512,2048]{1,0:T(8,128)} fusion(bf16[512,2048]{1,0:T(8,128)(2,1)} %collective-permute-done.10, bf16[512,4096]{1,0:T(8,128)(2,1)} %bitcast.98, bf16[4096,2048]{1,0:T(8,128)(2,1)} %all-gather.8.cloned.1.call-done), kind=kOutput, calls=%fused_computation.29 | convolution fusion | flops 8594128896 | bytes 27262976 | tf_op jit(solution)/shard_map/dot_general | solution.py:67
  535.8 5.4 copy.44
  541.2 2.7 fusion.19
  543.9 2.8 fusion.16
  546.8 2.1 fusion.17
  548.9 1.0 copy-done.3
  549.9 15.0 %multiply_reduce_fusion = (f32[512,32]{0,1:T(8,128)S(1)}, f32[512,32,64]{0,2,1:T(8,128)S(1)}) fusion(f32[512,32,64]{0,2,1:T(8,128)} %bitcast.96, bf16[512,32,64]{0,2,1:T(8,128)(2,1)S(1)} %bitcast.103, f32[32]{0:T(128)S(1)} %copy-done.17, f32[512,32]{0,1:T(8,128)S(1)} %copy-done.12, f32[512,32,64]{0,2,1:T(8,128)S(1)} %copy-done.3, ...), kind=kOutput, calls=%fused_computation.16 | convolution fusion | flops 1145028608 | bytes 29098112 | tf_op jit(solution)/shard_map/hts,shp->thp/dot_general | solution.py:85
  565.4 2.4 copy.45
  (70 shorter events, 7.3 us)
Async XLA Ops:
  6.5 277.2 %copy-start = (f32[512,32]{0,1:T(8,128)S(1)}, f32[512,32]{0,1:T(8,128)}, u32[]{:S(2)}) copy-start(f32[512,32]{0,1:T(8,128)} %param.13) | copy-start | bytes 196612
  6.5 262.4 %all-gather.4.cloned.1.call-start = ((), (), s32[]{:S(2)}) async-start(), calls=%async_computation.1 | async-start | bytes 20971520 | tf_op jit(solution)/shard_map/all_gather | solution.py:54
  7.3 392.7 %all-gather.8.cloned.1.call-start = ((), (), s32[]{:S(2)}) async-start(), calls=%async_computation.3 | async-start | bytes 20971520 | tf_op jit(solution)/shard_map/all_gather | solution.py:62
  8.0 28.1 %all-to-all-start = ((bf16[4,128,2048]{2,1,0:T(8,128)(2,1)}), bf16[4,128,2048]{2,1,0:T(8,128)(2,1)S(1)}, u32[]{:S(2)}, u32[]{:S(2)}) async-start(bf16[4,128,2048]{2,1,0:T(8,128)(2,1)} %bitcast.101), calls=%async_computation | async-start | bytes 4194304 | tf_op jit(solution)/shard_map/all_to_all | solution.py:55
  11.6 535.1 %all-gather.6.cloned.1.call-start = ((), (), s32[]{:S(2)}) async-start(), calls=%async_computation.2 | async-start | bytes 1310720 | tf_op jit(solution)/shard_map/all_gather | solution.py:111
  36.1 1.3 copy-start.2
  40.7 48.2 %collective-permute-start = (bf16[128,4096]{0,1:T(8,128)(2,1)S(1)}, bf16[128,4096]{0,1:T(8,128)(2,1)S(1)}, u32[]{:S(2)}, u32[]{:S(2)}) collective-permute-start(bf16[128,4096]{0,1:T(8,128)(2,1)S(1)} %get-tuple-element.20), channel_id=1, source_target_pairs={{0,16},{4,20},{8,24},{12,28},{16,0},{20,4},{24,8},{28,12},{1,17},{... | collective-permute-start | bytes 3145736 | tf_op jit(solution)/shard_map/ppermute | solution.py:59
  90.5 45.5 %collective-permute-start.1 = (bf16[1,2,128,4096]{2,3,1,0:T(8,128)(2,1)}, bf16[1,2,128,4096]{2,3,1,0:T(8,128)(2,1)}, u32[]{:S(2)}, u32[]{:S(2)}) collective-permute-start(bf16[1,2,128,4096]{2,3,1,0:T(8,128)(2,1)} %get-tuple-element.18), channel_id=1, source_target_pairs={{0,1},{1,0},{2,3},{3,2},{4,5},{5,4},{6,7},{7,6},{8,9},{9,8},{10,11... | collective-permute-start | bytes 6291464 | tf_op jit(solution)/shard_map/ppermute | solution.py:23
  142.4 89.6 %collective-permute-start.2 = (bf16[2,2,128,4096]{2,3,1,0:T(8,128)(2,1)}, bf16[2,2,128,4096]{2,3,1,0:T(8,128)(2,1)}, u32[]{:S(2)}, u32[]{:S(2)}) collective-permute-start(bf16[2,2,128,4096]{2,3,1,0:T(8,128)(2,1)} %get-tuple-element.14), channel_id=1, source_target_pairs={{0,2},{1,3},{2,0},{3,1},{4,6},{5,7},{6,4},{7,5},{8,10},{9,11},{10,... | collective-permute-start | bytes 12582920 | tf_op jit(solution)/shard_map/ppermute | solution.py:23
  269.0 20.6 %copy-start.5 = (bf16[512,2,4,256]{3,2,1,0:T(4,128)(2,1)S(1)}, bf16[512,2,4,256]{3,2,1,0:T(4,128)(2,1)}, u32[]{:S(2)}) copy-start(bf16[512,2,4,256]{3,2,1,0:T(4,128)(2,1)} %param.12) | copy-start | bytes 6291460
  283.8 91.2 %collective-permute-start.3 = (bf16[512,2048]{1,0:T(8,128)(2,1)}, bf16[512,2048]{1,0:T(8,128)(2,1)}, u32[]{:S(2)}, u32[]{:S(2)}) collective-permute-start(bf16[512,2048]{1,0:T(8,128)(2,1)} %convolution_convert_fusion.1), channel_id=1, source_target_pairs={{0,16},{4,20},{8,24},{12,28},{16,0},{20,4},{24,8},{28,12},{1,17},{... | collective-permute-start | bytes 6291464 | tf_op jit(solution)/shard_map/ppermute | solution.py:66
  285.1 5.7 copy-start.16
  285.9 128.7 %collective-permute-start.5 = (f32[32]{0:T(128)}, f32[32]{0:T(128)}, u32[]{:S(2)}, u32[]{:S(2)}) collective-permute-start(f32[32]{0:T(128)} %slice_reduce_fusion.1), channel_id=1, source_target_pairs={{0,4},{4,0},{8,12},{12,8},{16,20},{20,16},{24,28},{28,24},{1,5},{5... | collective-permute-start | bytes 392 | tf_op jit(solution)/shard_map/ppermute | solution.py:31
  389.8 2.9 copy-start.15
  392.7 4.3 copy-start.6
  396.9 18.4 %collective-permute-start.4 = (bf16[32,64,256]{2,1,0:T(8,128)(2,1)}, bf16[32,64,256]{2,1,0:T(8,128)(2,1)S(1)}, u32[]{:S(2)}, u32[]{:S(2)}) collective-permute-start(bf16[32,64,256]{2,1,0:T(8,128)(2,1)} %get-tuple-element.35), channel_id=1, source_target_pairs={{0,4},{4,0},{8,12},{12,8},{16,20},{20,16},{24,28},{28,24},{1,5},{5... | collective-permute-start | bytes 3145736 | tf_op jit(solution)/shard_map/ppermute | solution.py:31
  399.9 15.4 %copy-start.8 = (f32[32,64,256]{2,1,0:T(8,128)S(1)}, f32[32,64,256]{2,1,0:T(8,128)}, u32[]{:S(2)}) copy-start(f32[32,64,256]{2,1,0:T(8,128)} %get-tuple-element.36) | copy-start | bytes 6291460
  414.6 2.6 copy-start.10
  414.6 105.6 %collective-permute-start.10 = (bf16[512,2048]{1,0:T(8,128)(2,1)}, bf16[512,2048]{1,0:T(8,128)(2,1)}, u32[]{:S(2)}, u32[]{:S(2)}) collective-permute-start(bf16[512,2048]{1,0:T(8,128)(2,1)} %convolution_convert_fusion), channel_id=1, source_target_pairs={{0,16},{4,20},{8,24},{12,28},{16,0},{20,4},{24,8},{28,12},{1,17},{... | collective-permute-start | bytes 6291464 | tf_op jit(solution)/shard_map/ppermute | solution.py:66
  415.9 92.9 %copy-start.4 = (f32[32,64,256]{2,1,0:T(8,128)S(1)}, f32[32,64,256]{2,1,0:T(8,128)}, u32[]{:S(2)}) copy-start(f32[32,64,256]{2,1,0:T(8,128)} %param.15) | copy-start | bytes 6291460
  415.9 89.2 %collective-permute-start.6 = (bf16[32,64,256]{2,1,0:T(8,128)(2,1)S(1)}, bf16[32,64,256]{2,1,0:T(8,128)(2,1)S(1)}, u32[]{:S(2)}, u32[]{:S(2)}) collective-permute-start(bf16[32,64,256]{2,1,0:T(8,128)(2,1)S(1)} %get-tuple-element.9), channel_id=1, source_target_pairs={{0,8},{4,12},{8,0},{12,4},{16,24},{20,28},{24,16},{28,20},{1,9},{5... | collective-permute-start | bytes 3145736 | tf_op jit(solution)/shard_map/ppermute | solution.py:31
  419.3 64.3 %collective-permute-start.7 = (f32[32]{0:T(128)S(1)}, f32[32]{0:T(128)S(1)}, u32[]{:S(2)}, u32[]{:S(2)}) collective-permute-start(f32[32]{0:T(128)S(1)} %get-tuple-element.8), channel_id=1, source_target_pairs={{0,8},{4,12},{8,0},{12,4},{16,24},{20,28},{24,16},{28,20},{1,9},{5... | collective-permute-start | bytes 392 | tf_op jit(solution)/shard_map/ppermute | solution.py:31
  484.7 20.4 %collective-permute-start.9 = (f32[32]{0:T(128)S(1)}, f32[32]{0:T(128)S(1)}, u32[]{:S(2)}, u32[]{:S(2)}) collective-permute-start(f32[32]{0:T(128)S(1)} %get-tuple-element.32), channel_id=1, source_target_pairs={{0,16},{4,20},{8,24},{12,28},{16,0},{20,4},{24,8},{28,12},{1,17},{... | collective-permute-start | bytes 392 | tf_op jit(solution)/shard_map/ppermute | solution.py:31
  505.6 13.9 %collective-permute-start.8 = (bf16[8,64,256]{2,1,0:T(8,128)(2,1)S(1)}, bf16[8,64,256]{2,1,0:T(8,128)(2,1)S(1)}, u32[]{:S(2)}, u32[]{:S(2)}) collective-permute-start(bf16[8,64,256]{2,1,0:T(8,128)(2,1)S(1)} %select_convert_fusion.4), channel_id=1, source_target_pairs={{0,16},{4,20},{8,24},{12,28},{16,0},{20,4},{24,8},{28,12},{1,17},{... | collective-permute-start | bytes 786440 | tf_op jit(solution)/shard_map/ppermute | solution.py:31
  519.5 0.7 copy-start.11
  543.9 5.0 copy-start.9
  546.7 2.2 copy-start.7
  546.7 2.2 copy-start.12
  546.7 3.2 copy-start.3
  546.7 3.2 copy-start.13
  546.7 3.1 copy-start.14
  546.7 3.1 copy-start.17
  564.9 2.9 copy-start.1
Sparse Core Ops, SparseCore 0:
  8.9 171.6 all-gather.3
  182.1 192.6 all-gather.7
  520.3 18.5 all-gather.5
